TPU v7x, 512 devices: a whole 4x4x16 slice. The times are simulated.
512 devices in a mesh: batch: 64 (over z_lo, y, core), space: 8 (over x, z_hi).
Axes of the slice: x: 4, y: 4, z: 16 (z_hi: 2, z_lo: 8; z = z_hi * 8 + z_lo), core: 2. Of those that a mesh axis runs over, the one named last changes fastest.
Arguments:
- acts: bfloat16 [64, 32, 64, 640], P('batch', 'space'), may hold values from -6 to 6
- conv_weight: bfloat16 [5760, 640], P('batch', 'space'), may hold values from -0.078125 to 0.078125
- conv_bias: float32 [640], replicated, may hold values from -4 to 4
- out_cotangent: bfloat16 [64, 32, 64, 640], P('batch', 'space'), may hold values from -6 to 6
- basis_in: bfloat16 [5760, 64], P('batch'), may hold values from -0.078125 to 0.078125
- basis_out: bfloat16 [640, 64], P('batch'), may hold values from -0.25 to 0.25
- query_ids: int32 [8], replicated, may hold values from 0 to 63
Outputs:
- activated: bfloat16 [64, 32, 64, 640], P('batch', 'space')
- basis_in_new: bfloat16 [5760, 64], P('batch')
- scores: float32 [8, 64], P(None, 'batch')
All inputs are finite; a program needn't handle non-finite values.
Results may differ from a plain program's by a relative error of at most 0.0031.
Values may be sent and summed in bfloat16 or wider, within the bound.
No kernel may reach another device: no remote copies, remote signals or barrier semaphores. Data moves between devices by JAX's collectives and lax.ppermute only.
A program may use at most 64 MiB of HBM per device.

v0:
```python
import math
import jax
import jax.numpy as jnp
from jax import lax
from jax.sharding import PartitionSpec as P

DAMPING = 0.1


def extended(value, sides, width):
    for axis, dim in sides:
        size, length = (lax.axis_size(axis), value.shape[dim])
        up = [(i, (i + 1) % size) for i in range(size - 1)]
        down = [(j, i) for i, j in up]
        last = lax.slice_in_dim(value, length - width, length, axis=dim)
        initial = lax.slice_in_dim(value, 0, width, axis=dim)
        before = lax.ppermute(last, axis, up)
        after = lax.ppermute(initial, axis, down)
        value = jnp.concatenate([before, value, after], axis=dim)
    return value


def add_columns(segment, operand):
    return jnp.dot(operand, segment, preferred_element_type=jnp.float32)


def add_with_norms(segment, operand):
    summed = add_columns(segment, operand)
    squares = jnp.sum(jnp.square(segment.astype(jnp.float32)), axis=0)
    return (summed, squares)


def contract_rows(left_side, right_side):
    return lax.dot_general(
        left_side, right_side, (((0,), (0,)), ((), ())), preferred_element_type=jnp.float32
    )


def per_device(acts, conv_weight, conv_bias, out_cotangent, basis_in, basis_out, query_ids):
    ex_local, band_rows, band_cols, channels = acts.shape
    padded = extended(acts, (("space", 1),), 1)
    padded = jnp.pad(padded, ((0, 0), (0, 0), (1, 1), (0, 0)))
    shifted = [
        padded[:, row_shift : row_shift + band_rows, col_shift : col_shift + band_cols, :]
        for row_shift in range(3)
        for col_shift in range(3)
    ]
    positions = ex_local * band_rows * band_cols
    patches = jnp.stack(shifted, axis=3).reshape(positions, 9 * channels)
    kernel_cols = lax.all_gather(conv_weight, "batch", axis=0, tiled=True)
    preact = jnp.dot(
        patches,
        lax.all_gather(kernel_cols, "space", axis=1, tiled=True),
        preferred_element_type=jnp.float32,
    )
    preact = preact + conv_bias
    sigmoid_pre = jax.nn.sigmoid(preact)
    activated = (preact * sigmoid_pre).astype(jnp.bfloat16).reshape(acts.shape)
    grad_pre = (
        out_cotangent.reshape(positions, channels).astype(jnp.float32)
        * sigmoid_pre
        * (1.0 + preact * (1.0 - sigmoid_pre))
    ).astype(jnp.bfloat16)
    basis_rank = basis_in.shape[1]
    probe_in = add_columns(lax.all_gather(basis_in, "batch", axis=0, tiled=True), patches).astype(
        jnp.bfloat16
    )
    probe_out = add_columns(
        lax.all_gather(basis_out, "batch", axis=0, tiled=True), grad_pre
    ).astype(jnp.bfloat16)
    term_in = contract_rows(patches, probe_in)
    term_out = contract_rows(grad_pre, probe_out)
    summed = lax.psum((term_in, term_out), "space")
    owned_in, owned_out = (
        lax.psum_scatter(summed[0], "batch", scatter_dimension=0, tiled=True),
        lax.psum_scatter(summed[1], "batch", scatter_dimension=0, tiled=True),
    )
    total_positions = positions * lax.axis_size("batch") * lax.axis_size("space")
    basis_in_new = (owned_in / total_positions).astype(jnp.bfloat16)
    basis_out_new = (owned_out / total_positions).astype(jnp.bfloat16)
    raw_in, square_in = add_with_norms(
        lax.all_gather(basis_in_new, "batch", axis=0, tiled=True), patches
    )
    raw_out, square_out = add_with_norms(
        lax.all_gather(basis_out_new, "batch", axis=0, tiled=True), grad_pre
    )
    scale_in = jnp.sqrt(square_in)
    scale_out = jnp.sqrt(square_out)
    feat_in = (
        (raw_in / scale_in)
        .astype(jnp.bfloat16)
        .reshape(ex_local, band_rows * band_cols, basis_rank)
    )
    feat_out = (
        (raw_out / scale_out)
        .astype(jnp.bfloat16)
        .reshape(ex_local, band_rows * band_cols, basis_rank)
    )
    height = band_rows * lax.axis_size("space")
    projected = (
        jnp.einsum("epi,epj->eij", feat_out, feat_in, preferred_element_type=jnp.float32) / height
    )
    projected = lax.psum(projected, "space")
    scaled = projected / (scale_out[:, None] * scale_in[None, :] + DAMPING)
    all_projs = lax.all_gather(projected, "batch", axis=0, tiled=True)
    queries = jnp.take(all_projs, query_ids, axis=0)
    scores = jnp.einsum("qij,eij->qe", queries, scaled, precision=lax.Precision.HIGHEST) / (
        basis_rank * math.sqrt(basis_rank)
    )
    return (activated, basis_in_new, scores)


def solution(mesh):
    return jax.shard_map(
        per_device,
        mesh=mesh,
        in_specs=(
            P("batch", "space", None, None),
            P("batch", "space"),
            P(),
            P("batch", "space", None, None),
            P("batch", None),
            P("batch", None),
            P(),
        ),
        out_specs=(P("batch", "space", None, None), P("batch", None), P(None, "batch")),
        check_vma=False,
    )
```

profile of v0, /device:TPU:1, one launch (start us, length us, event | category | flops | bytes accessed | tf_op | source)
XLA Modules:
  0.0 1847.2 jit_solution(3337683036946885710)
XLA Ops:
  7.2 132.7 %all-gather = bf16[64,90,80]{1,2,0:T(8,128)(2,1)S(1)} all-gather(bf16[1,90,80]{1,2,0:T(8,128)(2,1)} %bitcast.90), channel_id=1, replica_groups=mesh['batch'=64,'space'=8] {'batch'}, dimensions={0}, use_global_device_ids=true | all-gather | bytes 936000 | tf_op jit(solution)/shard_map/all_gather | solution.py:50
  140.3 2.8 reshape.103
  143.2 8.0 collective-permute-start
  151.2 1.3 collective-permute-start.1
  152.5 167.6 %all-gather.1 = bf16[64,90,64]{1,2,0:T(8,128)(2,1)S(1)} all-gather(bf16[1,90,64]{1,2,0:T(8,128)(2,1)S(1)} %bitcast.91), channel_id=1, replica_groups=mesh['batch'=64,'space'=8] {'batch'}, dimensions={0}, use_global_device_ids=true | all-gather | bytes 748800 | tf_op jit(solution)/shard_map/all_gather | solution.py:65
  320.1 165.3 %all-gather.2 = bf16[64,10,64]{2,1,0:T(8,128)(2,1)S(1)} all-gather(bf16[1,10,64]{2,1,0:T(8,128)(2,1)S(1)} %bitcast.92), channel_id=1, replica_groups=mesh['batch'=64,'space'=8] {'batch'}, dimensions={0}, use_global_device_ids=true | all-gather | bytes 83200 | tf_op jit(solution)/shard_map/all_gather | solution.py:69
  486.2 2.4 reshape.105
  490.9 2.0 copy.14
  493.7 4.5 fusion.3
  498.3 6.4 fusion.11
  504.7 1.3 fusion.2
  506.1 1.3 dynamic-slice
  508.6 821.8 %all-reduce.7.cloned.1.call-done = (f32[5760,64]{0,1:T(8,128)}, f32[640,64]{1,0:T(8,128)}) async-done(((f32[5760,64]{0,1:T(8,128)}, f32[640,64]{1,0:T(8,128)}), (f32[5760,64]{0,1:T(8,128)}, f32[640,64]{1,0:T(8,128)})) %all-reduce.7.cloned.1.call-update) | async-done | bytes 1638416
  1332.0 66.9 %all-reduce.4 = (f32[90,64]{0,1:T(8,128)S(1)}, f32[10,64]{1,0:T(8,128)S(1)}) all-reduce(f32[90,64]{0,1:T(8,128)S(1)} %constant_dynamic-slice_fusion.1, f32[10,64]{1,0:T(8,128)S(1)} %constant_dynamic-slice_fusion), channel_id=1, replica_groups=mesh['batch'=64,'space'=8] {'space'}, use_global_device_ids=true, to_apply=%region_0.1 | all-reduce | flops 6400 | bytes 51200 | tf_op jit(solution)/shard_map/psum | solution.py:73
  1398.9 130.7 %all-gather.4 = bf16[64,90,64]{1,2,0:T(8,128)(2,1)S(1)} all-gather(bf16[1,90,64]{1,2,0:T(8,128)(2,1)S(1)} %fusion.45), channel_id=1, replica_groups=mesh['batch'=64,'space'=8] {'batch'}, dimensions={0}, use_global_device_ids=true | all-gather | bytes 748800 | tf_op jit(solution)/shard_map/all_gather | solution.py:82
  1529.6 1.6 copy.17
  1531.2 3.1 reshape.111
  1534.4 1.4 multiply_reduce_fusion
  1535.8 114.8 %all-gather.3 = bf16[64,10,64]{2,1,0:T(8,128)(2,1)S(1)} all-gather(bf16[1,10,64]{2,1,0:T(8,128)(2,1)S(1)} %fusion.29), channel_id=1, replica_groups=mesh['batch'=64,'space'=8] {'batch'}, dimensions={0}, use_global_device_ids=true | all-gather | bytes 83200 | tf_op jit(solution)/shard_map/all_gather | solution.py:85
  1653.5 2.3 fusion.6
  1655.7 60.8 %psum.23 = f32[1,64,64]{2,1,0:T(8,128)} all-reduce(f32[1,64,64]{2,1,0:T(8,128)S(1)} %fusion.6), channel_id=1, replica_groups=mesh['batch'=64,'space'=8] {'space'}, use_global_device_ids=true, to_apply=%region_6.7 | all-reduce | flops 4096 | bytes 32768 | tf_op jit(solution)/shard_map/psum | solution.py:103
  1718.1 119.1 %all-gather.10.cloned.1.call-done = f32[64,64,64]{2,1,0:T(8,128)} async-done(((f32[1,64,64]{2,1,0:T(8,128)}), f32[64,64,64]{2,1,0:T(8,128)}) %all-gather.10.cloned.1.call-update) | async-done | bytes 1048592 | tf_op jit(solution)/shard_map/all_gather | solution.py:105
  1837.2 2.2 gather_fusion
  1839.5 1.2 fusion.8
  (55 shorter events, 10.5 us)
Async XLA Ops:
  7.2 491.1 %all-gather.8.cloned.1.call-start = ((), (), s32[]{:S(2)}) async-start(), calls=%async_computation | async-start | bytes 8294400 | tf_op jit(solution)/shard_map/all_gather | solution.py:53
  139.9 3.2 copy-start
  139.9 12.6 copy-start.4
  140.0 180.1 %copy-start.5 = (bf16[10,64]{1,0:T(8,128)(2,1)S(1)}, bf16[10,64]{1,0:T(8,128)(2,1)}, u32[]{:S(2)}) copy-start(bf16[10,64]{1,0:T(8,128)(2,1)} %param.12) | copy-start | bytes 3844
  143.1 1187.3 %all-reduce.7.cloned.1.call-start = ((), (), s32[]{:S(2)}) async-start(), calls=%async_computation.2 | async-start | bytes 3604480
  143.2 345.4 %collective-permute-start = (bf16[1,1,64,640]{3,2,1,0:T(8,128)(2,1)S(1)}, bf16[1,1,64,640]{3,2,1,0:T(8,128)(2,1)S(1)}, u32[]{:S(2)}, u32[]{:S(2)}) collective-permute-start(bf16[1,1,64,640]{3,2,1,0:T(8,128)(2,1)S(1)} %get-tuple-element.9), channel_id=1, source_target_pairs={{0,1},{1,2},{2,3},{3,4},{4,5},{5,6},{6,7},{8,9},{9,10},{10,11},{11... | collective-permute-start | bytes 245768 | tf_op jit(solution)/shard_map/ppermute | solution.py:17
  151.2 337.4 %collective-permute-start.1 = (bf16[1,1,64,640]{3,2,1,0:T(8,128)(2,1)S(1)}, bf16[1,1,64,640]{3,2,1,0:T(8,128)(2,1)S(1)}, u32[]{:S(2)}, u32[]{:S(2)}) collective-permute-start(bf16[1,1,64,640]{3,2,1,0:T(8,128)(2,1)S(1)} %get-tuple-element.10), channel_id=1, source_target_pairs={{1,0},{2,1},{3,2},{4,3},{5,4},{6,5},{7,6},{9,8},{10,9},{11,10},{12... | collective-permute-start | bytes 245768 | tf_op jit(solution)/shard_map/ppermute | solution.py:18
  488.6 0.6 copy-start.1
  493.7 4.6 copy-start.6
  506.0 1331.2 %all-gather.10.cloned.1.call-start = ((), (), s32[]{:S(2)}) async-start(), calls=%async_computation.1 | async-start | bytes 2129920 | tf_op jit(solution)/shard_map/all_gather | solution.py:105
  1398.9 136.8 %copy-start.2 = (f32[90,64]{0,1:T(8,128)}, f32[90,64]{0,1:T(8,128)S(1)}, u32[]{:S(2)}) copy-start(f32[90,64]{0,1:T(8,128)S(1)} %get-tuple-element.5) | copy-start | bytes 69124
  1534.4 182.2 %copy-start.7 = (s32[8]{0:T(128)S(1)}, s32[8]{0:T(128)}, u32[]{:S(2)}) copy-start(s32[8]{0:T(128)} %param.13) | copy-start | bytes 100
  1651.3 65.3 %copy-start.3 = (f32[90,64]{0,1:T(8,128)S(1)}, f32[90,64]{0,1:T(8,128)}, u32[]{:S(2)}) copy-start(f32[90,64]{0,1:T(8,128)} %copy-done.2) | copy-start | bytes 69124
Sparse Core Ops, SparseCore 0:
  143.2 265.6 all-gather.7
  506.1 824.2 all-reduce.6
  1716.7 120.4 all-gather.9
where the time goes:
time: 1850 us
  waiting for transfers between devices  941 us (51%)
  blocking collectives  839 us (45%)
  local copies, waits for them, and re-layouts  20.8 us (1%)
    unnamed x4, waiting for transfers between devices  822 us
    all_gather x1, blocking collectives, per_device(): lax.all_gather(basis_in, 'batch', axis=0, tiled=True)  168 us
    all_gather x1, blocking collectives, per_device(): lax.all_gather(basis_out, 'batch', axis=0, tiled=True)  165 us
    all_gather x1, blocking collectives, per_device(): kernel_cols = lax.all_gather(conv_weight, 'batch', axis=0, tiled=True)  133 us
    all_gather x1, blocking collectives, per_device(): lax.all_gather(basis_in_new, 'batch', axis=0, tiled=True)  131 us
    all_gather x1, waiting for transfers between devices, per_device(): all_projs = lax.all_gather(projected, 'batch', axis=0, tiled=True)  119 us
    all_gather x1, blocking collectives, per_device(): lax.all_gather(basis_out_new, 'batch', axis=0, tiled=True)  115 us
    psum x1, blocking collectives, per_device(): summed = lax.psum((term_in, term_out), 'space')  66.9 us
  transfers between devices with their start and end apart: 5, of which 2 were waited for; matrix products, arithmetic and copies ran while one was open for 1% of the time, Pallas kernels for 0%

commit v1 on v0

--- a/solution.py
+++ b/solution.py
@@ -100,7 +100,7 @@
     projected = (
         jnp.einsum("epi,epj->eij", feat_out, feat_in, preferred_element_type=jnp.float32) / height
     )
-    projected = lax.psum(projected, "space")
+    projected = jnp.sum(lax.all_gather(projected, "space"), axis=0)
     scaled = projected / (scale_out[:, None] * scale_in[None, :] + DAMPING)
     all_projs = lax.all_gather(projected, "batch", axis=0, tiled=True)
     queries = jnp.take(all_projs, query_ids, axis=0)

time: 1850 us -> 1840 us (level)
    psum x1 -> x0, blocking collectives: 60.8 us -> none  [per_device(): projected = lax.psum(projected, 'space')]
    all_gather x0 -> x1, blocking collectives: none -> 57.2 us  [per_device(): projected = jnp.sum(lax.all_gather(projected, 'space'), axis=0)]
where the time goes in v1:
time: 1840 us
  waiting for transfers between devices  936 us (51%)
  blocking collectives  836 us (45%)
  local copies, waits for them, and re-layouts  20.8 us (1%)
    unnamed x4, waiting for transfers between devices  822 us
    all_gather x1, blocking collectives, per_device(): lax.all_gather(basis_in, 'batch', axis=0, tiled=True)  168 us
    all_gather x1, blocking collectives, per_device(): lax.all_gather(basis_out, 'batch', axis=0, tiled=True)  165 us
    all_gather x1, blocking collectives, per_device(): kernel_cols = lax.all_gather(conv_weight, 'batch', axis=0, tiled=True)  133 us
    all_gather x1, blocking collectives, per_device(): lax.all_gather(basis_in_new, 'batch', axis=0, tiled=True)  131 us
    all_gather x1, blocking collectives, per_device(): lax.all_gather(basis_out_new, 'batch', axis=0, tiled=True)  115 us
    all_gather x1, waiting for transfers between devices, per_device(): all_projs = lax.all_gather(projected, 'batch', axis=0, tiled=True)  114 us
    psum x1, blocking collectives, per_device(): summed = lax.psum((term_in, term_out), 'space')  66.9 us
  transfers between devices with their start and end apart: 5, of which 2 were waited for; matrix products, arithmetic and copies ran while one was open for 1% of the time, Pallas kernels for 0%

profile of v1, /device:TPU:1, one launch (start us, length us, event | category | flops | bytes accessed | tf_op | source)
XLA Modules:
  0.0 1839.6 jit_solution(14985259563659888838)
XLA Ops:
  7.2 132.7 %all-gather.2 = bf16[64,90,80]{1,2,0:T(8,128)(2,1)S(1)} all-gather(bf16[1,90,80]{1,2,0:T(8,128)(2,1)} %bitcast.91), channel_id=1, replica_groups=mesh['batch'=64,'space'=8] {'batch'}, dimensions={0}, use_global_device_ids=true | all-gather | bytes 936000 | tf_op jit(solution)/shard_map/all_gather | solution.py:50
  140.3 2.8 reshape.79
  143.2 8.0 collective-permute-start
  151.2 1.3 collective-permute-start.1
  152.5 167.6 %all-gather.3 = bf16[64,90,64]{1,2,0:T(8,128)(2,1)S(1)} all-gather(bf16[1,90,64]{1,2,0:T(8,128)(2,1)S(1)} %bitcast.92), channel_id=1, replica_groups=mesh['batch'=64,'space'=8] {'batch'}, dimensions={0}, use_global_device_ids=true | all-gather | bytes 748800 | tf_op jit(solution)/shard_map/all_gather | solution.py:65
  320.1 165.3 %all-gather.4 = bf16[64,10,64]{2,1,0:T(8,128)(2,1)S(1)} all-gather(bf16[1,10,64]{2,1,0:T(8,128)(2,1)S(1)} %bitcast.93), channel_id=1, replica_groups=mesh['batch'=64,'space'=8] {'batch'}, dimensions={0}, use_global_device_ids=true | all-gather | bytes 83200 | tf_op jit(solution)/shard_map/all_gather | solution.py:69
  486.2 2.4 reshape.81
  490.9 2.0 copy.14
  493.7 4.5 fusion.3
  498.3 6.4 fusion.10
  504.7 1.3 fusion.2
  506.1 1.3 dynamic-slice
  508.6 821.8 %all-reduce.7.cloned.1.call-done = (f32[5760,64]{0,1:T(8,128)}, f32[640,64]{1,0:T(8,128)}) async-done(((f32[5760,64]{0,1:T(8,128)}, f32[640,64]{1,0:T(8,128)}), (f32[5760,64]{0,1:T(8,128)}, f32[640,64]{1,0:T(8,128)})) %all-reduce.7.cloned.1.call-update) | async-done | bytes 1638416
  1332.0 66.9 %all-reduce.4 = (f32[90,64]{0,1:T(8,128)S(1)}, f32[10,64]{1,0:T(8,128)S(1)}) all-reduce(f32[90,64]{0,1:T(8,128)S(1)} %constant_dynamic-slice_fusion.1, f32[10,64]{1,0:T(8,128)S(1)} %constant_dynamic-slice_fusion), channel_id=1, replica_groups=mesh['batch'=64,'space'=8] {'space'}, use_global_device_ids=true, to_apply=%region_0.1 | all-reduce | flops 6400 | bytes 51200 | tf_op jit(solution)/shard_map/psum | solution.py:73
  1398.9 130.7 %all-gather.6 = bf16[64,90,64]{1,2,0:T(8,128)(2,1)S(1)} all-gather(bf16[1,90,64]{1,2,0:T(8,128)(2,1)S(1)} %fusion.44), channel_id=1, replica_groups=mesh['batch'=64,'space'=8] {'batch'}, dimensions={0}, use_global_device_ids=true | all-gather | bytes 748800 | tf_op jit(solution)/shard_map/all_gather | solution.py:82
  1529.6 1.6 copy.17
  1531.2 3.1 reshape.87
  1534.4 1.4 multiply_reduce_fusion
  1535.8 115.3 %all-gather.5 = bf16[64,10,64]{2,1,0:T(8,128)(2,1)S(1)} all-gather(bf16[1,10,64]{2,1,0:T(8,128)(2,1)S(1)} %fusion.28), channel_id=1, replica_groups=mesh['batch'=64,'space'=8] {'batch'}, dimensions={0}, use_global_device_ids=true | all-gather | bytes 83200 | tf_op jit(solution)/shard_map/all_gather | solution.py:85
  1654.0 2.3 fusion.5
  1656.2 57.2 %all-gather = f32[512,64]{1,0:T(8,128)S(1)} all-gather(f32[64,64]{1,0:T(8,128)S(1)} %fusion.5), channel_id=2, replica_groups=mesh['batch'=64,'space'=8] {'space'}, dimensions={0}, use_global_device_ids=true | all-gather | bytes 147456 | tf_op jit(solution)/shard_map/all_gather | solution.py:103
  1715.7 113.9 %all-gather.12.cloned.1.call-done = f32[4096,64]{1,0:T(8,128)} async-done(((f32[64,64]{1,0:T(8,128)}), f32[4096,64]{1,0:T(8,128)}) %all-gather.12.cloned.1.call-update) | async-done | bytes 1048592 | tf_op jit(solution)/shard_map/all_gather | solution.py:105
  1829.6 2.2 gather_fusion
  1831.8 1.2 fusion.7
  (56 shorter events, 11.2 us)
Async XLA Ops:
  7.2 491.1 %all-gather.10.cloned.1.call-start = ((), (), s32[]{:S(2)}) async-start(), calls=%async_computation | async-start | bytes 8294400 | tf_op jit(solution)/shard_map/all_gather | solution.py:53
  139.9 3.2 copy-start
  139.9 12.6 copy-start.4
  140.0 180.1 %copy-start.5 = (bf16[10,64]{1,0:T(8,128)(2,1)S(1)}, bf16[10,64]{1,0:T(8,128)(2,1)}, u32[]{:S(2)}) copy-start(bf16[10,64]{1,0:T(8,128)(2,1)} %param.12) | copy-start | bytes 3844
  143.1 1187.3 %all-reduce.7.cloned.1.call-start = ((), (), s32[]{:S(2)}) async-start(), calls=%async_computation.2 | async-start | bytes 3604480
  143.2 345.4 %collective-permute-start = (bf16[1,1,64,640]{3,2,1,0:T(8,128)(2,1)S(1)}, bf16[1,1,64,640]{3,2,1,0:T(8,128)(2,1)S(1)}, u32[]{:S(2)}, u32[]{:S(2)}) collective-permute-start(bf16[1,1,64,640]{3,2,1,0:T(8,128)(2,1)S(1)} %get-tuple-element.9), channel_id=1, source_target_pairs={{0,1},{1,2},{2,3},{3,4},{4,5},{5,6},{6,7},{8,9},{9,10},{10,11},{11... | collective-permute-start | bytes 245768 | tf_op jit(solution)/shard_map/ppermute | solution.py:17
  151.2 337.4 %collective-permute-start.1 = (bf16[1,1,64,640]{3,2,1,0:T(8,128)(2,1)S(1)}, bf16[1,1,64,640]{3,2,1,0:T(8,128)(2,1)S(1)}, u32[]{:S(2)}, u32[]{:S(2)}) collective-permute-start(bf16[1,1,64,640]{3,2,1,0:T(8,128)(2,1)S(1)} %get-tuple-element.10), channel_id=1, source_target_pairs={{1,0},{2,1},{3,2},{4,3},{5,4},{6,5},{7,6},{9,8},{10,9},{11,10},{12... | collective-permute-start | bytes 245768 | tf_op jit(solution)/shard_map/ppermute | solution.py:18
  488.6 0.6 copy-start.1
  493.7 4.6 copy-start.6
  506.0 1323.5 %all-gather.12.cloned.1.call-start = ((), (), s32[]{:S(2)}) async-start(), calls=%async_computation.1 | async-start | bytes 2129920 | tf_op jit(solution)/shard_map/all_gather | solution.py:105
  1398.9 136.8 %copy-start.2 = (f32[90,64]{0,1:T(8,128)}, f32[90,64]{0,1:T(8,128)S(1)}, u32[]{:S(2)}) copy-start(f32[90,64]{0,1:T(8,128)S(1)} %get-tuple-element.5) | copy-start | bytes 69124
  1535.7 178.4 %copy-start.7 = (s32[8]{0:T(128)S(1)}, s32[8]{0:T(128)}, u32[]{:S(2)}) copy-start(s32[8]{0:T(128)} %param.13) | copy-start | bytes 100
  1651.8 62.4 %copy-start.3 = (f32[90,64]{0,1:T(8,128)S(1)}, f32[90,64]{0,1:T(8,128)}, u32[]{:S(2)}) copy-start(f32[90,64]{0,1:T(8,128)} %copy-done.2) | copy-start | bytes 69124
Sparse Core Ops, SparseCore 0:
  143.2 265.6 all-gather.9
  506.1 824.2 all-reduce.6
  1714.3 115.2 all-gather.11
